TPU v7x, 32 devices: a whole 2x2x4 slice. The times are simulated.
32 devices in a mesh: req: 2 (over y), seq: 4 (over z), branch: 2 (over core), tp: 2 (over x).
Axes of the slice: x: 2, y: 2, z: 4, core: 2. Of those that a mesh axis runs over, the one named last changes fastest.
Arguments:
- projected: bfloat16 [2, 768, 3, 4096], P('branch', ('req', 'seq', 'tp')), parts along dimension 1, may hold values from -24 to 24
- hint_gain: float32 [4096], replicated, may hold values from 0.3 to 1.5
- block_map: int32 [4], replicated, may hold values from 0 to 3, each once
- token_perm: int32 [8, 48], replicated, may hold values from 0 to 47, each once within a row
Outputs:
- combined: bfloat16 [2, 768, 4096], P('branch', ('req', 'seq', 'tp')), parts along dimension 1
There are 2 independent parts, one for each index of `req`. A program takes and returns all parts, laid end to end along the dimension named above; an argument that names none is the same for every part. Nothing has to cross between parts.
Inputs may be any that keep to these rules, and one draw needn't show every extreme that they name: `block_map`: a permutation of the 4 sequence shards. `token_perm`: each row is a permutation of 0 to 47.
All inputs are finite; a program needn't handle non-finite values.
Results may differ from a plain program's by a relative error of at most 0.0055.
Values may be sent and summed in bfloat16 or wider, within the bound.
A program may use at most 64 MiB of HBM per device.

v0:
```python
import math

import jax
import jax.numpy as jnp
from jax import lax
from jax.sharding import PartitionSpec as P

HD = 128


key_block = 512


def passed_along(x, axis, by):
    count = lax.axis_size(axis)
    pairs = [(i, i + by) for i in range(count) if 0 <= i + by < count]
    return lax.ppermute(x, axis, pairs)


def attend(queries, key_rows, value_rows):
    row_count, columns = queries.shape
    local_heads = columns // HD
    query_heads = queries.reshape(row_count, local_heads, HD)
    scaling = 1.0 / math.sqrt(HD)
    initial = (
        jnp.full((local_heads, row_count), -jnp.inf, jnp.float32),
        jnp.zeros((local_heads, row_count), jnp.float32),
        jnp.zeros((local_heads, row_count, HD), jnp.float32),
    )
    running = initial
    key_piece = lax.all_gather(key_rows, "tp", axis=0, tiled=True)
    value_piece = lax.all_gather(value_rows, "tp", axis=0, tiled=True)
    length = key_piece.shape[0]
    step_rows = key_block if length % key_block == 0 else length
    number = length // step_rows
    key_blocks = key_piece.reshape(number, step_rows, local_heads, HD)
    value_blocks = value_piece.reshape(number, step_rows, local_heads, HD)

    def update(carried, blocks_now):
        highest, totals, summed = carried
        key_now, value_now = blocks_now
        scores = (
            jnp.einsum("qhd,khd->hqk", query_heads, key_now, preferred_element_type=jnp.float32)
            * scaling
        )
        new_highest = jnp.maximum(highest, jnp.max(scores, axis=2))
        fading = jnp.exp(highest - new_highest)
        weights = jnp.exp(scores - new_highest[..., None])
        totals = totals * fading + jnp.sum(weights, axis=2)
        summed = summed * fading[..., None] + jnp.einsum(
            "hqk,khd->hqd",
            weights.astype(jnp.bfloat16),
            value_now,
            preferred_element_type=jnp.float32,
        )
        return ((new_highest, totals, summed), None)

    running, unused = lax.scan(update, running, (key_blocks, value_blocks))
    highest, totals, summed = running
    result = summed / totals[..., None]
    return jnp.transpose(result, (1, 0, 2)).reshape(row_count, columns).astype(jnp.bfloat16)


def to_tokens(head_rows):
    return lax.all_to_all(head_rows, "seq", split_axis=0, concat_axis=1, tiled=True)


def on_device(projected, hint_gain, block_map, token_perm):
    block_rows = projected.shape[1]
    features = projected.shape[3]
    seq_count = lax.axis_size("seq")
    tp_count = lax.axis_size("tp")
    branch_index = lax.axis_index("branch")
    seq_index = lax.axis_index("seq")
    tp_index = lax.axis_index("tp")
    arrived = lax.all_to_all(projected[0], "seq", split_axis=2, concat_axis=0, tiled=True)
    columns = features // seq_count
    attended = attend(arrived[:, 0], arrived[:, 1], arrived[:, 2])
    attended = lax.optimization_barrier(attended)
    partner = passed_along(attended, "branch", -1)
    perm_table = token_perm.reshape(seq_count, tp_count, block_rows)
    column = lax.dynamic_index_in_dim(perm_table, tp_index, 1, keepdims=False)
    picked = (block_map[:, None] * block_rows + column).reshape(-1)
    control = jnp.take(partner, picked, axis=0).astype(jnp.float32)
    gain_slice = lax.dynamic_slice_in_dim(hint_gain, seq_index * columns, columns)
    summed = (attended.astype(jnp.float32) + gain_slice * control).astype(jnp.bfloat16)
    result = to_tokens(jnp.where(branch_index == 0, summed, attended))
    return result[None]


def solution(mesh):
    return jax.shard_map(
        on_device,
        mesh=mesh,
        in_specs=(P("branch", ("req", "seq", "tp"), None, None), P(), P(), P()),
        out_specs=P("branch", ("req", "seq", "tp"), None),
        check_vma=False,
    )
```

profile of v0, /device:TPU:0, one launch (start us, length us, event | category | flops | bytes accessed | tf_op | source)
XLA Modules:
  0.0 113.4 jit_solution(10417822175712787521)
XLA Ops:
  0.0 6.2 %copy.21 = bf16[1,48,3,4096]{1,2,3,0:T(4,128)(2,1)} copy(bf16[1,48,3,4096]{3,1,2,0:T(8,128)(2,1)} %param.4) | data formatting | bytes 2359296 | tf_op args[0]
  6.2 5.3 %bitcast_bitcast_fusion = bf16[4096,3,48]{2,1,0:T(4,128)(2,1)} fusion(bf16[1,48,3,4096]{1,2,3,0:T(4,128)(2,1)} %copy.21), kind=kLoop, calls=%fused_computation.28 | loop fusion | bytes 2359296
  11.5 6.9 %reshape.89 = bf16[4,2,73728]{2,1,0:T(2,128)(2,1)} reshape(bf16[4096,3,48]{2,1,0:T(4,128)(2,1)} %bitcast_bitcast_fusion) | data formatting | bytes 2359296
  18.4 6.5 %all-to-all-start = ((bf16[4,2,73728]{2,1,0:T(2,128)(2,1)}), bf16[4,2,73728]{2,1,0:T(2,128)(2,1)S(1)}, u32[]{:S(2)}, u32[]{:S(2)}) async-start(bf16[4,2,73728]{2,1,0:T(2,128)(2,1)} %reshape.89), calls=%async_computation | async-start | bytes 2359296 | tf_op jit(solution)/shard_map/all_to_all | solution.py:76
  24.8 0.5 broadcast.77
  25.4 0.7 fusion.13
  26.0 0.6 squeeze.30
  26.7 0.1 add.74
  26.7 0.6 add.80
  27.4 26.0 %all-to-all-done = bf16[4,2,73728]{2,1,0:T(2,128)(2,1)S(1)} async-done(((bf16[4,2,73728]{2,1,0:T(2,128)(2,1)}), bf16[4,2,73728]{2,1,0:T(2,128)(2,1)S(1)}, u32[]{:S(2)}, u32[]{:S(2)}) %all-to-all-start) | async-done | bytes 1179680 | tf_op jit(solution)/shard_map/all_to_all | solution.py:76
  53.4 6.3 %reshape.90 = bf16[4096,3,48]{2,1,0:T(4,128)(2,1)} reshape(bf16[4,2,73728]{2,1,0:T(2,128)(2,1)S(1)} %all-to-all-done) | data formatting | bytes 2359296
  59.7 5.4 %copy.23 = bf16[4,48,3,1024]{3,1,0,2:T(8,128)(2,1)S(1)} copy(bf16[4,48,3,1024]{1,2,3,0:T(4,128)(2,1)} %bitcast.45) | data formatting | bytes 2359296 | tf_op jit(solution)/shard_map/all_to_all | solution.py:76
  65.1 0.1 slice_bitcast_fusion
  65.2 10.8 %all-gather = bf16[384,1,1024]{2,0,1:T(8,128)(2,1)S(1)} all-gather(bf16[192,1,1024]{2,0,1:T(8,128)(2,1)S(1)} %get-tuple-element.28), channel_id=2, replica_groups=mesh['req'=2,'seq'=4,'branch'=2,'tp'=2] {'tp'}, dimensions={0}, use_global_device_ids=true | all-gather | bytes 1179648 | tf_op jit(solution)/shard_map/all_gather | solution.py:31
  76.0 0.4 copy.24
  76.4 0.6 multiply_reduce_fusion
  77.0 0.6 multiply_bitcast_fusion
  77.6 0.8 fusion
  78.4 0.6 bitcast_add_fusion
  79.0 9.9 %all-gather.1 = bf16[384,1,1024]{2,0,1:T(8,128)(2,1)S(1)} all-gather(bf16[192,1,1024]{2,0,1:T(8,128)(2,1)S(1)} %get-tuple-element.20), channel_id=3, replica_groups=mesh['req'=2,'seq'=4,'branch'=2,'tp'=2] {'tp'}, dimensions={0}, use_global_device_ids=true | all-gather | bytes 1179648 | tf_op jit(solution)/shard_map/all_gather | solution.py:32
  88.9 1.2 %copy.27 = bf16[384,1,1024]{0,2,1:T(8,128)(2,1)} copy(bf16[384,1,1024]{2,0,1:T(8,128)(2,1)S(1)} %all-gather.1) | data formatting | bytes 1572864 | tf_op jit(solution)/shard_map/all_gather | solution.py:32
  90.1 2.3 %fusion.5 = bf16[8,24,8,128]{3,2,1,0:T(8,128)(2,1)S(1)} fusion(bf16[384,8,128]{0,2,1:T(8,128)(2,1)} %bitcast.53, f32[8,192,384]{2,1,0:T(8,128)S(1)} %get-tuple-element.32, f32[8,192]{1,0:T(8,128)S(1)} %get-tuple-element.30, f32[192,8]{0,1:T(8,128)} %bitcast_add_fusion, f32[192,8]{0,1:T(8,128)} %multiply_bitcast_fusion), kind=kOutput, calls=%fused_computation.9 | convolution fusion | flops 153354240 | bytes 3557376 | tf_op jit(solution)/shard_map/while/body/eval_jaxpr/hqk,khd->hqd/dot_general | solution.py:50
  92.4 0.1 copy.42
  92.5 1.3 %collective-permute-start = (bf16[192,1024]{1,0:T(8,128)(2,1)S(1)}, bf16[192,1024]{1,0:T(8,128)(2,1)S(1)}, u32[]{:S(2)}, u32[]{:S(2)}) collective-permute-start(bf16[192,1024]{1,0:T(8,128)(2,1)S(1)} %bitcast.50), channel_id=1, source_target_pairs={{2,0},{3,1},{6,4},{7,5},{10,8},{11,9},{14,12},{15,13},{18,16},{19,... | collective-permute-start | bytes 1179656 | tf_op jit(solution)/shard_map/ppermute | solution.py:17
  93.9 0.1 add.75
  93.9 0.1 squeeze.29
  94.0 2.1 %collective-permute-done = bf16[192,1024]{1,0:T(8,128)(2,1)S(1)} collective-permute-done((bf16[192,1024]{1,0:T(8,128)(2,1)S(1)}, bf16[192,1024]{1,0:T(8,128)(2,1)S(1)}, u32[]{:S(2)}, u32[]{:S(2)}) %collective-permute-start) | collective-permute-done | bytes 393248 | tf_op jit(solution)/shard_map/ppermute | solution.py:17
  96.1 1.0 gather_fusion
  97.2 0.3 fusion.9
  97.4 14.7 %all_to_all.34 = bf16[4,48,1024]{2,1,0:T(8,128)(2,1)S(1)} all-to-all(bf16[4,48,1024]{2,1,0:T(8,128)(2,1)S(1)} %bitcast.52), channel_id=1, replica_groups=mesh['req'=2,'seq'=4,'branch'=2,'tp'=2] {'seq'}, dimensions={0} | all-to-all | bytes 786432 | tf_op jit(solution)/shard_map/all_to_all | solution.py:65
  112.1 0.3 copy.30
  112.4 1.0 broadcast_in_dim.31
  (15 shorter events, 0.1 us)
Async XLA Ops:
  18.4 7.0 %copy-start.2 = (s32[8,48]{1,0:T(8,128)S(1)}, s32[8,48]{1,0:T(8,128)}, u32[]{:S(2)}) copy-start(s32[8,48]{1,0:T(8,128)} %param.7) | copy-start | bytes 4612
  18.4 8.3 %copy-start.3 = (s32[4]{0:T(128)S(1)}, s32[4]{0:T(128)}, u32[]{:S(2)}) copy-start(s32[4]{0:T(128)} %param.6) | copy-start | bytes 52
  18.4 35.0 %all-to-all-start = ((bf16[4,2,73728]{2,1,0:T(2,128)(2,1)}), bf16[4,2,73728]{2,1,0:T(2,128)(2,1)S(1)}, u32[]{:S(2)}, u32[]{:S(2)}) async-start(bf16[4,2,73728]{2,1,0:T(2,128)(2,1)} %reshape.89), calls=%async_computation | async-start | bytes 2359296 | tf_op jit(solution)/shard_map/all_to_all | solution.py:76
  90.1 3.7 %copy-start = (s32[192,1]{0,1:T(1,128)S(1)}, s32[192,1]{0,1:T(1,128)}, u32[]{:S(2)}) copy-start(s32[192,1]{0,1:T(1,128)} %squeeze.30) | copy-start | bytes 2308
  90.1 3.7 %copy-start.1 = (s32[192,1]{0,1:T(1,128)S(1)}, s32[192,1]{0,1:T(1,128)}, u32[]{:S(2)}) copy-start(s32[192,1]{0,1:T(1,128)} %add.80) | copy-start | bytes 2308
  92.5 3.6 %collective-permute-start = (bf16[192,1024]{1,0:T(8,128)(2,1)S(1)}, bf16[192,1024]{1,0:T(8,128)(2,1)S(1)}, u32[]{:S(2)}, u32[]{:S(2)}) collective-permute-start(bf16[192,1024]{1,0:T(8,128)(2,1)S(1)} %bitcast.50), channel_id=1, source_target_pairs={{2,0},{3,1},{6,4},{7,5},{10,8},{11,9},{14,12},{15,13},{18,16},{19,... | collective-permute-start | bytes 1179656 | tf_op jit(solution)/shard_map/ppermute | solution.py:17
  94.0 3.1 %dynamic-slice-start = ((f32[4096]{0:T(1024)}, s32[]{:T(128)}), f32[1024]{0:T(1024)S(1)}, s32[]{:S(2)}) async-start(f32[4096]{0:T(1024)} %param.5, s32[]{:T(128)} %select_n.36), calls=%async_computation.2 | async-start | bytes 8704 | tf_op jit(solution)/shard_map/dynamic_slice | solution.py:85
where the time goes:
time: 114 us; the launch traced here: 113 us
  local copies, waits for them, and re-layouts  36.8 us (32%)
  blocking collectives  35.4 us (31%)
  waiting for transfers between devices  28.1 us (25%)
  starting transfers between devices  7.77 us (7%)
  matrix products  2.88 us (3%)
  other arithmetic  2.32 us (2%)
    all_to_all x1, waiting for transfers between devices, on_device(): lax.all_to_all(projected[0], 'seq', split_axis=2, concat_axis=0, tiled=True)  26 us
    unnamed x14, local copies, waits for them, and re-layouts  24.8 us
    all_to_all x1, blocking collectives, to_tokens(): lax.all_to_all(head_rows, 'seq', split_axis=0, concat_axis=1, tiled=True)  14.7 us
    all_gather x1, blocking collectives, attend(): key_piece = lax.all_gather(key_rows, 'tp', axis=0, tiled=True)  10.8 us
    all_gather x1, blocking collectives, attend(): value_piece = lax.all_gather(value_rows, 'tp', axis=0, tiled=True)  9.92 us
    all_to_all x1, starting transfers between devices, on_device(): lax.all_to_all(projected[0], 'seq', split_axis=2, concat_axis=0, tiled=True)  6.48 us
    all_to_all x1, local copies, waits for them, and re-layouts, on_device(): lax.all_to_all(projected[0], 'seq', split_axis=2, concat_axis=0, tiled=True)  5.4 us
    dot_general x1, matrix products, update(): jnp.einsum('hqk,khd->hqd', weights.astype(jnp.bfloat16), value_now, prefe...  2.3 us
  transfers between devices with their start and end apart: 2, of which 2 were waited for; matrix products, arithmetic and copies ran while one was open for 2% of the time, Pallas kernels for 0%

commit v1 on v0

--- a/solution.py
+++ b/solution.py
@@ -1,11 +1,15 @@
+import functools
 import math
 
 import jax
 import jax.numpy as jnp
 from jax import lax
+from jax.experimental import pallas as pl
+from jax.experimental.pallas import tpu as pltpu
 from jax.sharding import PartitionSpec as P
 
 HD = 128
+MESH = pl.DeviceIdType.MESH
 
 
 key_block = 512
@@ -88,9 +92,174 @@
     return result[None]
 
 
+def attend_whole(queries, key_rows, value_rows):
+    contract_last = (((1,), (1,)), ((), ()))
+    scores = lax.dot_general(
+        queries, key_rows, contract_last, preferred_element_type=jnp.float32
+    ) * (1.0 / math.sqrt(HD))
+    weights = jnp.exp(scores - jnp.max(scores, axis=1, keepdims=True))
+    totals = jnp.sum(weights, axis=1, keepdims=True)
+    summed = jnp.dot(
+        weights.astype(jnp.bfloat16), value_rows, preferred_element_type=jnp.float32
+    )
+    return (summed / totals).astype(jnp.bfloat16)
+
+
+def exchange_kernel(
+    seq_count, tp_count, chunks,
+    rows_ref, gain_ref, map_ref, perm_ref, out_ref,
+    arrived, attended, hint, pick,
+    in_send, in_recv, out_send, out_recv, hint_send, hint_recv,
+):
+    count = seq_count * tp_count
+    block = rows_ref.shape[1]
+    tokens = count * block
+    branch = lax.axis_index("branch")
+    me = lax.axis_index("seq") * tp_count + lax.axis_index("tp")
+
+    def peer(k):
+        return lax.rem(me + k, count)
+
+    def coords(device):
+        return {"seq": device // tp_count, "tp": lax.rem(device, tp_count)}
+
+    def head_columns(device, chunk):
+        return pl.ds(pl.multiple_of((device * chunks + chunk) * HD, HD), HD)
+
+    def block_rows(device):
+        return pl.ds(pl.multiple_of(device * block, block), block)
+
+    barrier = pltpu.get_barrier_semaphore()
+    for k in range(1, count):
+        pl.semaphore_signal(barrier, inc=1, device_id=coords(peer(k)), device_id_type=MESH)
+    pl.semaphore_signal(barrier, inc=1, device_id={"branch": 1 - branch}, device_id_type=MESH)
+    pl.semaphore_wait(barrier, count)
+
+    def in_copy(chunk, k):
+        source = rows_ref.at[:, :, head_columns(peer(k), chunk)]
+        target = arrived.at[chunk, :, block_rows(me), :]
+        if k == 0:
+            return pltpu.make_async_copy(source, target, in_recv.at[chunk, 0])
+        return pltpu.make_async_remote_copy(
+            src_ref=source, dst_ref=target,
+            send_sem=in_send.at[chunk, k], recv_sem=in_recv.at[chunk, k],
+            device_id=coords(peer(k)), device_id_type=MESH,
+        )
+
+    def out_copy(chunk, k):
+        source = attended.at[chunk, block_rows(peer(k)), :]
+        target = out_ref.at[:, head_columns(me, chunk)]
+        if k == 0:
+            return pltpu.make_async_copy(source, target, out_recv.at[chunk, 0])
+        return pltpu.make_async_remote_copy(
+            src_ref=source, dst_ref=target,
+            send_sem=out_send.at[chunk, k], recv_sem=out_recv.at[chunk, k],
+            device_id=coords(peer(k)), device_id_type=MESH,
+        )
+
+    def hint_copy(chunk):
+        return pltpu.make_async_remote_copy(
+            src_ref=attended.at[chunk], dst_ref=hint.at[chunk],
+            send_sem=hint_send.at[chunk], recv_sem=hint_recv.at[chunk],
+            device_id={"branch": 1 - branch}, device_id_type=MESH,
+        )
+
+    half = count // 2
+    order = sorted(range(count), key=lambda k: abs(k - half))
+    for chunk in range(chunks):
+        for k in order:
+            in_copy(chunk, k).start()
+
+    @pl.when(branch == 0)
+    def _():
+        square = (block, block)
+        diagonal = lax.broadcasted_iota(jnp.int32, square, 0) == lax.broadcasted_iota(jnp.int32, square, 1)
+        lane = lax.broadcasted_iota(jnp.int32, (block, tokens), 1).astype(jnp.float32)
+        for p in range(count):
+            first = (map_ref[p // tp_count] * tp_count + p % tp_count) * block
+            row = (perm_ref[p : p + 1, :] + first).astype(jnp.float32)
+            column = jnp.sum(jnp.where(diagonal, row, 0.0), axis=1, keepdims=True)
+            pick[p * block : (p + 1) * block, :] = jnp.where(lane == column, 1.0, 0.0).astype(jnp.bfloat16)
+
+    for chunk in range(chunks):
+        for k in order:
+            if k == 0:
+                in_copy(chunk, k).wait()
+            else:
+                in_copy(chunk, k).wait_recv()
+        result = attend_whole(arrived[chunk, 0], arrived[chunk, 1], arrived[chunk, 2])
+
+        @pl.when(branch == 1)
+        def _():
+            attended[chunk] = result
+            hint_copy(chunk).start()
+
+        @pl.when(branch == 0)
+        def _():
+            hint_copy(chunk).wait_recv()
+            control = jnp.dot(pick[...], hint[chunk], preferred_element_type=jnp.float32)
+            gain = gain_ref[pl.ds(me * chunks + chunk, 1), :]
+            attended[chunk] = (result.astype(jnp.float32) + gain * control).astype(jnp.bfloat16)
+
+        for k in order:
+            out_copy(chunk, k).start()
+
+    for chunk in range(chunks):
+        @pl.when(branch == 1)
+        def _():
+            hint_copy(chunk).wait_send()
+
+        for k in order:
+            if k == 0:
+                out_copy(chunk, k).wait()
+            else:
+                in_copy(chunk, k).wait_send()
+                out_copy(chunk, k).wait()
+
+
+def by_kernel(seq_count, tp_count, projected, hint_gain, block_map, token_perm):
+    count = seq_count * tp_count
+    block, features = projected.shape[1], projected.shape[3]
+    chunks = features // HD // count
+    tokens = count * block
+    rows = jnp.transpose(projected[0], (1, 0, 2))
+    dma = pltpu.SemaphoreType.DMA
+    out = pl.pallas_call(
+        functools.partial(exchange_kernel, seq_count, tp_count, chunks),
+        out_shape=jax.ShapeDtypeStruct((block, features), projected.dtype),
+        in_specs=[
+            pl.BlockSpec(memory_space=pl.ANY),
+            pl.BlockSpec(memory_space=pltpu.VMEM),
+            pl.BlockSpec(memory_space=pltpu.SMEM),
+            pl.BlockSpec(memory_space=pltpu.VMEM),
+        ],
+        out_specs=pl.BlockSpec(memory_space=pl.ANY),
+        scratch_shapes=[
+            pltpu.VMEM((chunks, 3, tokens, HD), projected.dtype),
+            pltpu.VMEM((chunks, tokens, HD), projected.dtype),
+            pltpu.VMEM((chunks, tokens, HD), projected.dtype),
+            pltpu.VMEM((tokens, tokens), jnp.bfloat16),
+            dma((chunks, count)), dma((chunks, count)),
+            dma((chunks, count)), dma((chunks, count)),
+            dma((chunks,)), dma((chunks,)),
+        ],
+        compiler_params=pltpu.CompilerParams(collective_id=0, has_side_effects=True),
+    )(rows, hint_gain.reshape(features // HD, HD), block_map, token_perm)
+    return out[None]
+
+
 def solution(mesh):
+    sizes = dict(mesh.shape)
+    count = sizes["seq"] * sizes["tp"]
+
+    def program(projected, hint_gain, block_map, token_perm):
+        heads = projected.shape[3] // HD
+        if heads % count == 0:
+            return by_kernel(sizes["seq"], sizes["tp"], projected, hint_gain, block_map, token_perm)
+        return on_device(projected, hint_gain, block_map, token_perm)
+
     return jax.shard_map(
-        on_device,
+        program,
         mesh=mesh,
         in_specs=(P("branch", ("req", "seq", "tp"), None, None), P(), P(), P()),
         out_specs=P("branch", ("req", "seq", "tp"), None),

time: 114 us -> 46.6 us (0.41)
  Pallas kernels: 0 us -> 44.6 us
  blocking collectives: 35.4 us -> 0 us
  local copies, waits for them, and re-layouts: 36.8 us -> 1.77 us
  waiting for transfers between devices: 28.1 us -> 0 us
  starting transfers between devices: 7.77 us -> 0 us
  matrix products: 2.88 us -> 0 us
  other arithmetic: 2.32 us -> 0 us
    pallas_call x0 -> x1, Pallas kernels: none -> 44.6 us  [by_kernel(): pl.pallas_call(functools.partial(exchange_kernel, seq_count, tp_count, ch...]
    all_to_all x1 -> x0, waiting for transfers between devices: 26 us -> none  [on_device(): lax.all_to_all(projected[0], 'seq', split_axis=2, concat_axis=0, tiled=True)]
    unnamed x14 -> x1, local copies, waits for them, and re-layouts: 24.8 us -> 1.77 us
    all_gather x2 -> x0, blocking collectives: 20.7 us -> none  [the longest x1 10.8 us: attend(): key_piece = lax.all_gather(key_rows, 'tp', axis=0, tiled=True)]
    all_to_all x1 -> x0, blocking collectives: 14.7 us -> none  [to_tokens(): lax.all_to_all(head_rows, 'seq', split_axis=0, concat_axis=1, tiled=True)]
    all_to_all x1 -> x0, starting transfers between devices: 6.48 us -> none  [on_device(): lax.all_to_all(projected[0], 'seq', split_axis=2, concat_axis=0, tiled=True)]
    all_to_all x2 -> x0, local copies, waits for them, and re-layouts: 5.71 us -> none  [the longest x1 5.4 us: on_device(): lax.all_to_all(projected[0], 'seq', split_axis=2, concat_axis=0, tiled=True)]
    dot_general x2 -> x0, matrix products: 2.88 us -> none  [the longest x1 2.3 us: update(): jnp.einsum('hqk,khd->hqd', weights.astype(jnp.bfloat16), value_now, prefe...]
  transfers between devices with their start and end apart: 2 -> 0, of which waited for: 2 -> 0; matrix products, arithmetic and copies ran while one was open for 2% -> 0% of each run, Pallas kernels for 0% -> 0%
where the time goes in v1:
time: 46.6 us; the launch traced here: 46.4 us
  Pallas kernels  44.6 us (96%)
  local copies, waits for them, and re-layouts  1.77 us (4%)
    pallas_call x1, Pallas kernels, by_kernel(): pl.pallas_call(functools.partial(exchange_kernel, seq_count, tp_count, ch...  44.6 us
    unnamed x1, local copies, waits for them, and re-layouts  1.77 us

profile of v1, /device:TPU:0, one launch (start us, length us, event | category | flops | bytes accessed | tf_op | source)
XLA Modules:
  0.0 46.4 jit_solution(9601609754073206910)
XLA Ops:
  0.0 44.6 %shard_map.46 = bf16[48,4096]{1,0:T(8,128)(2,1)} custom-call(bf16[3,48,4096]{2,1,0:T(8,128)(2,1)} %bitcast.6, f32[32,128]{1,0:T(8,128)} %bitcast.7, s32[4]{0:T(128)} %map_ref.1, s32[8,48]{1,0:T(8,128)} %perm_ref.1), custom_call_target="tpu_custom_call" | custom-call | tf_op jit(solution)/shard_map/pallas_call | solution.py:227
  44.6 1.8 %copy.6 = bf16[1,48,4096]{2,1,0:T(8,128)(2,1)} copy(bf16[1,48,4096]{2,1,0:T(8,128)(2,1)} %bitcast.5) | data formatting | bytes 786432

commit v2 on v1

--- a/solution.py
+++ b/solution.py
@@ -107,18 +107,27 @@
 
 def exchange_kernel(
     seq_count, tp_count, chunks,
-    rows_ref, gain_ref, map_ref, perm_ref, out_ref,
-    arrived, attended, hint, pick,
-    in_send, in_recv, out_send, out_recv, hint_send, hint_recv,
+    rows_ref, gain_in, map_in, perm_in, out_ref,
+    arrived, attended, hint, pick, gain_ref, map_ref, perm_ref,
+    in_send, in_recv, out_send, out_recv, hint_send, hint_recv, table_sem, from_above, from_below,
 ):
     count = seq_count * tp_count
     block = rows_ref.shape[1]
     tokens = count * block
     branch = lax.axis_index("branch")
-    me = lax.axis_index("seq") * tp_count + lax.axis_index("tp")
+    seq_index, tp_index = lax.axis_index("seq"), lax.axis_index("tp")
+    me = seq_index * tp_count + tp_index
+    half = seq_count // 2 if seq_count % 2 == 0 else seq_count
+    side, place = seq_index // half, lax.rem(seq_index, half)
+    sides = seq_count // half
 
     def peer(k):
-        return lax.rem(me + k, count)
+        across, turn, shift = k // (half * tp_count), k // tp_count % half, k % tp_count
+        there = lax.rem(side + across, sides) * half + lax.rem(place + turn, half)
+        return there * tp_count + lax.rem(tp_index + shift, tp_count)
+
+    def beside(shift):
+        return lax.rem(tp_index + shift, tp_count)
 
     def coords(device):
         return {"seq": device // tp_count, "tp": lax.rem(device, tp_count)}
@@ -129,21 +138,19 @@
     def block_rows(device):
         return pl.ds(pl.multiple_of(device * block, block), block)
 
-    barrier = pltpu.get_barrier_semaphore()
-    for k in range(1, count):
-        pl.semaphore_signal(barrier, inc=1, device_id=coords(peer(k)), device_id_type=MESH)
-    pl.semaphore_signal(barrier, inc=1, device_id={"branch": 1 - branch}, device_id_type=MESH)
-    pl.semaphore_wait(barrier, count)
-
-    def in_copy(chunk, k):
-        source = rows_ref.at[:, :, head_columns(peer(k), chunk)]
-        target = arrived.at[chunk, :, block_rows(me), :]
-        if k == 0:
-            return pltpu.make_async_copy(source, target, in_recv.at[chunk, 0])
+    def in_copy(chunk, device, origin):
         return pltpu.make_async_remote_copy(
-            src_ref=source, dst_ref=target,
-            send_sem=in_send.at[chunk, k], recv_sem=in_recv.at[chunk, k],
-            device_id=coords(peer(k)), device_id_type=MESH,
+            src_ref=rows_ref.at[:, :, head_columns(device, chunk)],
+            dst_ref=arrived.at[chunk, :, block_rows(me), :],
+            send_sem=in_send.at[chunk, device], recv_sem=in_recv.at[chunk, origin],
+            device_id=coords(device), device_id_type=MESH,
+        )
+
+    def own_in_copy(chunk):
+        return pltpu.make_async_copy(
+            rows_ref.at[:, :, head_columns(me, chunk)],
+            arrived.at[chunk, :, block_rows(me), :],
+            in_recv.at[chunk, me],
         )
 
     def out_copy(chunk, k):
@@ -164,14 +171,82 @@
             device_id={"branch": 1 - branch}, device_id_type=MESH,
         )
 
-    half = count // 2
-    order = sorted(range(count), key=lambda k: abs(k - half))
-    for chunk in range(chunks):
+    order = range(count - 1, -1, -1)
+    early = range(min(2, chunks))
+    below, above = seq_index > 0, seq_index < seq_count - 1
+
+    def send_row(row, shifts):
+        for chunk in early:
+            for shift in shifts:
+                in_copy(chunk, row * tp_count + beside(shift), me).start()
+
+    barrier = pltpu.get_barrier_semaphore()
+    pl.semaphore_signal(barrier, inc=1, device_id={"branch": 1 - branch}, device_id_type=MESH)
+    for shift in range(1, tp_count):
+        pl.semaphore_signal(barrier, inc=1, device_id={"tp": beside(shift)}, device_id_type=MESH)
+
+    @pl.when(below)
+    def _():
+        pl.semaphore_signal(barrier, inc=1, device_id={"seq": seq_index - 1}, device_id_type=MESH)
+
+    @pl.when(above)
+    def _():
+        pl.semaphore_signal(barrier, inc=1, device_id={"seq": seq_index + 1}, device_id_type=MESH)
+
+    reach = seq_count - 1
+    beside_count = (seq_index + reach) // seq_count + (reach - seq_index + reach) // seq_count
+    pl.semaphore_wait(barrier, tp_count + beside_count)
+
+    for away in range(1, seq_count):
+        @pl.when(below & (seq_index + away - 1 < seq_count))
+        def _():
+            pl.semaphore_signal(from_above.at[away], inc=1, device_id={"seq": seq_index - 1}, device_id_type=MESH)
+
+        @pl.when(above & (seq_index - away + 1 >= 0))
+        def _():
+            pl.semaphore_signal(from_below.at[away], inc=1, device_id={"seq": seq_index + 1}, device_id_type=MESH)
+
+        if away == 1:
+            @pl.when(above)
+            def _():
+                send_row(seq_index + 1, [0])
+
+            @pl.when(below)
+            def _():
+                send_row(seq_index - 1, [0])
+
+            send_row(seq_index, range(1, tp_count))
+            for chunk in range(chunks):
+                own_in_copy(chunk).start()
+
+        shifts = range(1 if away == 1 else 0, tp_count)
+
+        @pl.when(seq_index + away < seq_count)
+        def _():
+            pl.semaphore_wait(from_above.at[away], 1)
+            send_row(seq_index + away, shifts)
+
+        @pl.when(seq_index - away >= 0)
+        def _():
+            pl.semaphore_wait(from_below.at[away], 1)
+            send_row(seq_index - away, shifts)
+
+    for chunk in range(len(early), chunks):
         for k in order:
-            in_copy(chunk, k).start()
+            if k:
+                in_copy(chunk, peer(k), me).start()
 
     @pl.when(branch == 0)
     def _():
+        tables = [
+            pltpu.make_async_copy(gain_in, gain_ref, table_sem.at[0]),
+            pltpu.make_async_copy(map_in, map_ref, table_sem.at[1]),
+            pltpu.make_async_copy(perm_in, perm_ref, table_sem.at[2]),
+        ]
+        for table in tables:
+            table.start()
+        for table in tables:
+            table.wait()
         square = (block, block)
         diagonal = lax.broadcasted_iota(jnp.int32, square, 0) == lax.broadcasted_iota(jnp.int32, square, 1)
         lane = lax.broadcasted_iota(jnp.int32, (block, tokens), 1).astype(jnp.float32)
@@ -184,9 +259,9 @@
     for chunk in range(chunks):
         for k in order:
             if k == 0:
-                in_copy(chunk, k).wait()
+                own_in_copy(chunk).wait()
             else:
-                in_copy(chunk, k).wait_recv()
+                in_copy(chunk, peer(k), peer(k)).wait_recv()
         result = attend_whole(arrived[chunk, 0], arrived[chunk, 1], arrived[chunk, 2])
 
         @pl.when(branch == 1)
@@ -213,7 +288,7 @@
             if k == 0:
                 out_copy(chunk, k).wait()
             else:
-                in_copy(chunk, k).wait_send()
+                in_copy(chunk, peer(k), me).wait_send()
                 out_copy(chunk, k).wait()
 
 
@@ -227,21 +302,20 @@
     out = pl.pallas_call(
         functools.partial(exchange_kernel, seq_count, tp_count, chunks),
         out_shape=jax.ShapeDtypeStruct((block, features), projected.dtype),
-        in_specs=[
-            pl.BlockSpec(memory_space=pl.ANY),
-            pl.BlockSpec(memory_space=pltpu.VMEM),
-            pl.BlockSpec(memory_space=pltpu.SMEM),
-            pl.BlockSpec(memory_space=pltpu.VMEM),
-        ],
+        in_specs=[pl.BlockSpec(memory_space=pl.ANY)] * 4,
         out_specs=pl.BlockSpec(memory_space=pl.ANY),
         scratch_shapes=[
             pltpu.VMEM((chunks, 3, tokens, HD), projected.dtype),
             pltpu.VMEM((chunks, tokens, HD), projected.dtype),
             pltpu.VMEM((chunks, tokens, HD), projected.dtype),
             pltpu.VMEM((tokens, tokens), jnp.bfloat16),
+            pltpu.VMEM((features // HD, HD), hint_gain.dtype),
+            pltpu.SMEM(block_map.shape, block_map.dtype),
+            pltpu.VMEM(token_perm.shape, token_perm.dtype),
             dma((chunks, count)), dma((chunks, count)),
             dma((chunks, count)), dma((chunks, count)),
-            dma((chunks,)), dma((chunks,)),
+            dma((chunks,)), dma((chunks,)), dma((3,)),
+            pltpu.SemaphoreType.REGULAR((seq_count,)), pltpu.SemaphoreType.REGULAR((seq_count,)),
         ],
         compiler_params=pltpu.CompilerParams(collective_id=0, has_side_effects=True),
     )(rows, hint_gain.reshape(features // HD, HD), block_map, token_perm)

time: 46.6 us -> 44.2 us (0.948)
  Pallas kernels: 44.6 us -> 42.2 us
    pallas_call x1, Pallas kernels: 44.6 us -> 42.2 us  [by_kernel(): pl.pallas_call(functools.partial(exchange_kernel, seq_count, tp_count, ch...]
where the time goes in v2:
time: 44.2 us; the launch traced here: 44 us
  Pallas kernels  42.2 us (95%)
  local copies, waits for them, and re-layouts  1.77 us (4%)
    pallas_call x1, Pallas kernels, by_kernel(): pl.pallas_call(functools.partial(exchange_kernel, seq_count, tp_count, ch...  42.2 us
    unnamed x1, local copies, waits for them, and re-layouts  1.77 us

profile of v2, /device:TPU:0, one launch (start us, length us, event | category | flops | bytes accessed | tf_op | source)
XLA Modules:
  0.0 44.0 jit_solution(5552258789276312483)
XLA Ops:
  0.0 42.2 %shard_map.46 = bf16[48,4096]{1,0:T(8,128)(2,1)} custom-call(bf16[3,48,4096]{2,1,0:T(8,128)(2,1)} %bitcast.6, f32[32,128]{1,0:T(8,128)} %bitcast.7, s32[4]{0:T(128)} %map_in.1, s32[8,48]{1,0:T(8,128)} %perm_in.1), custom_call_target="tpu_custom_call" | custom-call | tf_op jit(solution)/shard_map/pallas_call | solution.py:302
  42.2 1.8 %copy.6 = bf16[1,48,4096]{2,1,0:T(8,128)(2,1)} copy(bf16[1,48,4096]{2,1,0:T(8,128)(2,1)} %bitcast.5) | data formatting | bytes 786432

commit v3 on v2

--- a/solution.py
+++ b/solution.py
@@ -172,7 +172,7 @@
         )
 
     order = range(count - 1, -1, -1)
-    early = range(min(2, chunks))
+    early = range(min(3, chunks))
     below, above = seq_index > 0, seq_index < seq_count - 1
 
     def send_row(row, shifts):
@@ -301,7 +301,7 @@
     dma = pltpu.SemaphoreType.DMA
     out = pl.pallas_call(
         functools.partial(exchange_kernel, seq_count, tp_count, chunks),
-        out_shape=jax.ShapeDtypeStruct((block, features), projected.dtype),
+        out_shape=pltpu.VMEM((block, features), projected.dtype),
         in_specs=[pl.BlockSpec(memory_space=pl.ANY)] * 4,
         out_specs=pl.BlockSpec(memory_space=pl.ANY),
         scratch_shapes=[

time: 44.2 us -> 42.8 us (0.968)
  local copies, waits for them, and re-layouts: 1.77 us -> 0.75 us
    unnamed x1, local copies, waits for them, and re-layouts: 1.77 us -> 0.75 us
where the time goes in v3:
time: 42.8 us; the launch traced here: 42.6 us
  Pallas kernels  41.9 us (98%)
  local copies, waits for them, and re-layouts  0.75 us (2%)
    pallas_call x1, Pallas kernels, by_kernel(): pl.pallas_call(functools.partial(exchange_kernel, seq_count, tp_count, ch...  41.9 us

profile of v3, /device:TPU:0, one launch (start us, length us, event | category | flops | bytes accessed | tf_op | source)
XLA Modules:
  0.0 42.6 jit_solution(9610372902448632464)
XLA Ops:
  0.0 41.9 %shard_map.46 = bf16[48,4096]{1,0:T(8,128)(2,1)S(1)} custom-call(bf16[3,48,4096]{2,1,0:T(8,128)(2,1)} %bitcast.6, f32[32,128]{1,0:T(8,128)} %bitcast.7, s32[4]{0:T(128)} %map_in.1, s32[8,48]{1,0:T(8,128)} %perm_in.1), custom_call_target="tpu_custom_call" | custom-call | tf_op jit(solution)/shard_map/pallas_call | solution.py:302
  41.9 0.7 %copy.6 = bf16[1,48,4096]{2,1,0:T(8,128)(2,1)} copy(bf16[1,48,4096]{2,1,0:T(8,128)(2,1)S(1)} %bitcast.5) | data formatting | bytes 786432
